TPU v7x, 256 devices: a whole 4x4x8 slice. The times are simulated.
256 devices in a mesh: dp: 64 (over z_hi, y, x), tensor: 4 (over z_lo, core).
Axes of the slice: x: 4, y: 4, z: 8 (z_hi: 4, z_lo: 2; z = z_hi * 2 + z_lo), core: 2. Of those that a mesh axis runs over, the one named last changes fastest.
Arguments:
- hidden: bfloat16 [32768, 8192], P('dp', 'tensor'), may hold values from -16 to 16
- kv_weight: bfloat16 [8192, 1024], P(None, 'tensor'), may hold values from -0.0625 to 0.0625
- queries: bfloat16 [32768, 4096], P('dp', 'tensor'), may hold values from -28 to 28
- out_grad: bfloat16 [32768, 4096], P('dp', 'tensor'), may hold values from -6 to 6
- live_blocks: int32 [64], P('dp'), may hold values from 0 to 4, as said below
- doc_start: int32 [32768], P('dp'), may hold values from 0 to 127, as said below
Outputs:
- q_grad: bfloat16 [32768, 4096], P('dp', 'tensor')
- hidden_grad: bfloat16 [32768, 8192], P('dp', 'tensor')
- kv_weight_grad: float32 [8192, 1024], P('dp', 'tensor')
Inputs may be any that keep to these rules, and one draw needn't show every extreme that they name: live_blocks[i] + live_blocks[j] = 4 for the two indices i and j of dp that lie half the axis apart; the live blocks of an index are its first ones. doc_start of a row is at most its own position within its block, position 0 of every block is 0, and the rows of one document are consecutive.
All inputs are finite; a program needn't handle non-finite values.
Results may differ from a plain program's by a relative error of at most 0.014.
The roundings to bfloat16 on the way count: a program that leaves them out, or rounds other values in their place, can miss the bound.
Values may be sent and summed in bfloat16 or wider, within the bound.
A program may use at most 128 MiB of HBM per device.

v0:
```python
import jax
import jax.numpy as jnp
from jax import lax
from jax.sharding import PartitionSpec as P

HEAD_DIM = 128
BLOCK = 128
NBLK = 4


def attend(query_rows, key_rows, value_rows, grad_rows, start_rows, live_slots):
    factor = HEAD_DIM ** (-0.5)
    position = jnp.arange(BLOCK)
    allowed = (
        (position[None, None, :] >= start_rows[:, :, None])
        & (position[None, None, :] <= position[None, :, None])
        & live_slots[:, None, None]
    )
    allowed = allowed[:, None, None]
    scores = (
        jnp.einsum("brkgd,bskd->bkgrs", query_rows, key_rows, preferred_element_type=jnp.float32)
        * factor
    )
    row_max = jnp.max(jnp.where(allowed, scores, -1e30), axis=-1, keepdims=True)
    weights = jnp.where(allowed, jnp.exp(scores - row_max), 0.0)
    row_sum = jnp.sum(weights, axis=-1, keepdims=True)
    row_sum = jnp.where(live_slots[:, None, None, None, None], row_sum, 1.0)
    prob_full = weights / row_sum
    prob_low = prob_full.astype(jnp.bfloat16)
    attended = jnp.einsum(
        "bkgrs,bskd->brkgd", prob_low, value_rows, preferred_element_type=jnp.float32
    ).astype(jnp.bfloat16)
    attended = lax.optimization_barrier(attended)
    row_dot = jnp.sum(grad_rows.astype(jnp.float32) * attended.astype(jnp.float32), axis=-1)
    prob_grad = jnp.einsum(
        "brkgd,bskd->bkgrs", grad_rows, value_rows, preferred_element_type=jnp.float32
    )
    score_grad = (
        prob_full * (prob_grad - jnp.transpose(row_dot, (0, 2, 3, 1))[..., None]) * factor
    ).astype(jnp.bfloat16)
    query_grad = jnp.einsum(
        "bkgrs,bskd->brkgd", score_grad, key_rows, preferred_element_type=jnp.float32
    ).astype(jnp.bfloat16)
    key_grad = jnp.einsum(
        "bkgrs,brkgd->bskd", score_grad, query_rows, preferred_element_type=jnp.float32
    ).astype(jnp.bfloat16)
    value_grad = jnp.einsum(
        "bkgrs,brkgd->bskd", prob_low, grad_rows, preferred_element_type=jnp.float32
    ).astype(jnp.bfloat16)
    return (query_grad, jnp.stack([key_grad, value_grad], axis=3))


def on_device(hidden, kv_weight, queries, out_grad, live_blocks, doc_start):
    row_count = hidden.shape[0]
    kv_cols = kv_weight.shape[1]
    kv_local = kv_cols // (2 * HEAD_DIM)
    group_size = queries.shape[1] // (kv_local * HEAD_DIM)
    gathered = lax.all_gather(hidden, "tensor", axis=1, tiled=True)
    key_value = jnp.dot(gathered, kv_weight, preferred_element_type=jnp.float32).astype(
        jnp.bfloat16
    )
    key_value = key_value.reshape(NBLK, BLOCK, kv_local, 2, HEAD_DIM)
    key_rows = key_value[:, :, :, 0]
    value_rows = key_value[:, :, :, 1]
    query_rows = queries.reshape(NBLK, BLOCK, kv_local, group_size, HEAD_DIM)
    grad_rows = out_grad.reshape(NBLK, BLOCK, kv_local, group_size, HEAD_DIM)
    start_rows = doc_start.reshape(NBLK, BLOCK)
    live_count = live_blocks[0]
    query_grad, kv_grad = attend(
        query_rows, key_rows, value_rows, grad_rows, start_rows, jnp.arange(NBLK) < live_count
    )
    q_grad = query_grad.reshape(row_count, queries.shape[1])
    kv_grad = kv_grad.reshape(row_count, kv_cols)
    partial_value = lax.dot_general(
        kv_grad, kv_weight, (((1,), (1,)), ((), ())), preferred_element_type=jnp.float32
    )
    hidden_grad = lax.psum_scatter(
        partial_value.astype(jnp.bfloat16), "tensor", scatter_dimension=1, tiled=True
    )
    weight_grad = lax.psum_scatter(
        lax.dot_general(
            gathered, kv_grad, (((0,), (0,)), ((), ())), preferred_element_type=jnp.float32
        ),
        "dp",
        scatter_dimension=0,
        tiled=True,
    )
    return (q_grad, hidden_grad, weight_grad)


def solution(mesh):
    in_specs = (
        P("dp", "tensor"),
        P(None, "tensor"),
        P("dp", "tensor"),
        P("dp", "tensor"),
        P("dp"),
        P("dp"),
    )
    out_specs = (P("dp", "tensor"), P("dp", "tensor"), P("dp", "tensor"))
    return jax.shard_map(
        on_device, mesh=mesh, in_specs=in_specs, out_specs=out_specs, check_vma=False
    )
```

profile of v0, /device:TPU:1, one launch (start us, length us, event | category | flops | bytes accessed | tf_op | source)
XLA Modules:
  0.0 614.5 jit_solution(17390597814734032298)
XLA Ops:
  7.2 0.7 all-gather.2.cloned.1.call-update
  8.9 1.2 copy.49
  10.4 1.8 copy.50
  12.2 1.9 copy.26
  14.3 83.8 %all-gather.2.cloned.1.call-done = bf16[512,8192]{1,0:T(8,128)(2,1)} async-done(((bf16[512,2048]{1,0:T(8,128)(2,1)}), bf16[512,8192]{1,0:T(8,128)(2,1)}) %all-gather.2.cloned.1.call-update) | async-done | bytes 8388624 | tf_op jit(solution)/shard_map/all_gather | solution.py:58
  98.0 7.6 %convolution_convert_fusion.3 = bf16[512,256]{1,0:T(8,128)(2,1)} fusion(bf16[512,8192]{1,0:T(8,128)(2,1)} %all-gather.2.cloned.1.call-done, bf16[8192,256]{1,0:T(8,128)(2,1)} %param.7), kind=kOutput, calls=%fused_computation.20 | convolution fusion | flops 2147614720 | bytes 12845056 | tf_op jit(solution)/shard_map/dot_general | solution.py:59
  105.7 1.0 reshape.122
  107.1 0.5 fusion.3
  107.6 0.5 fusion.7
  108.4 0.7 fusion.13
  109.1 0.8 fusion.8
  110.3 0.9 fusion.10
  111.3 0.4 fusion.14
  112.0 0.5 slice-done
  112.5 1.3 slice-done.1
  113.8 5.8 convolution_bitcast_fusion
  119.8 7.8 %convolution_convert_fusion = bf16[512,8192]{1,0:T(8,128)(2,1)} fusion(bf16[8192,256]{1,0:T(8,128)(2,1)} %param.7, bf16[64,8,2,128]{3,2,1,0:T(2,128)(2,1)S(1)} %bitcast.155), kind=kOutput, calls=%fused_computation | convolution fusion | flops 2151677952 | bytes 12845056 | tf_op jit(solution)/shard_map/dot_general | solution.py:74
  127.6 0.9 copy-done.4
  128.6 0.5 fusion.9
  129.1 0.7 copy.29
  129.8 1.2 copy.80
  131.0 353.3 %reduce-scatter.5.cloned.1.call-done = f32[128,256]{0,1:T(8,128)} async-done(((f32[8192,256]{0,1:T(8,128)}), f32[128,256]{0,1:T(8,128)}) %reduce-scatter.5.cloned.1.call-update) | async-done | bytes 131088 | tf_op jit(solution)/shard_map/reduce_scatter | solution.py:80
  484.4 1.7 copy.33
  486.0 122.0 %reduce-scatter.3.cloned.1.call-done = bf16[512,2048]{1,0:T(8,128)(2,1)} async-done(((bf16[512,8192]{1,0:T(8,128)(2,1)}), bf16[512,2048]{1,0:T(8,128)(2,1)}) %reduce-scatter.3.cloned.1.call-update) | async-done | bytes 2097168 | tf_op jit(solution)/shard_map/reduce_scatter | solution.py:77
  (29 shorter events, 2.3 us)
Async XLA Ops:
  7.2 1.4 copy-start.1
  7.2 1.7 copy-start
  7.2 90.9 %all-gather.2.cloned.1.call-start = ((), (), s32[]{:S(2)}) async-start(), calls=%async_computation.2 | async-start | bytes 10485760 | tf_op jit(solution)/shard_map/all_gather | solution.py:58
  7.9 476.4 %reduce-scatter.5.cloned.1.call-start = ((), (), s32[]{:S(2)}) async-start(), calls=%async_computation.4 | async-start | bytes 8519680 | tf_op jit(solution)/shard_map/reduce_scatter | solution.py:80
  12.2 2.0 copy-start.5
  107.0 1.0 copy-start.3
  107.1 1.3 copy-start.2
  110.3 2.2 slice-start
  110.3 3.5 slice-start.1
  119.6 488.4 %reduce-scatter.3.cloned.1.call-start = ((), (), s32[]{:S(2)}) async-start(), calls=%async_computation.3 | async-start | bytes 10485760 | tf_op jit(solution)/shard_map/reduce_scatter | solution.py:77
  127.6 0.9 copy-start.4
Sparse Core Ops, SparseCore 0:
  9.8 88.2 all-gather.1
  119.7 364.6 reduce-scatter.4
  487.6 120.4 reduce-scatter.2
where the time goes:
time: 615 us
  waiting for transfers between devices  560 us (91%)
  matrix products  25.1 us (4%)
  between operations  14.6 us (2%)
  local copies, waits for them, and re-layouts  13.5 us (2%)
    reduce_scatter x1, waiting for transfers between devices, on_device(): lax.psum_scatter(lax.dot_general(gathered, kv_grad, (((0,), (0,)), ((), (...  353 us
    reduce_scatter x1, waiting for transfers between devices, on_device(): lax.psum_scatter(partial_value.astype(jnp.bfloat16), 'tensor', scatter_di...  122 us
    all_gather x1, waiting for transfers between devices, on_device(): gathered = lax.all_gather(hidden, 'tensor', axis=1, tiled=True)  83.8 us
  transfers between devices with their start and end apart: 3, of which 3 were waited for; matrix products, arithmetic and copies ran while one was open for 3% of the time, Pallas kernels for 0%

commit v1 on v0

--- a/solution.py
+++ b/solution.py
@@ -55,7 +55,9 @@
     kv_cols = kv_weight.shape[1]
     kv_local = kv_cols // (2 * HEAD_DIM)
     group_size = queries.shape[1] // (kv_local * HEAD_DIM)
-    gathered = lax.all_gather(hidden, "tensor", axis=1, tiled=True)
+    gathered = jnp.concatenate(
+        lax.all_to_all(jnp.stack([hidden] * lax.axis_size("tensor")), "tensor", 0, 0), axis=1
+    )
     key_value = jnp.dot(gathered, kv_weight, preferred_element_type=jnp.float32).astype(
         jnp.bfloat16
     )

time: 615 us -> 636 us (1.034)
  starting transfers between devices: 0.3 us -> 9.19 us
    all_to_all x0 -> x1, waiting for transfers between devices: none -> 85.6 us  [on_device(): lax.all_to_all(jnp.stack([hidden] * lax.axis_size('tensor')), 'tensor', 0...]
    all_gather x1 -> x0, waiting for transfers between devices: 83.8 us -> none  [on_device(): gathered = lax.all_gather(hidden, 'tensor', axis=1, tiled=True)]
    all_to_all x0 -> x1, starting transfers between devices: none -> 8.96 us  [on_device(): lax.all_to_all(jnp.stack([hidden] * lax.axis_size('tensor')), 'tensor', 0...]
where the time goes in v1:
time: 636 us; the launch traced here: 635 us
  waiting for transfers between devices  563 us (89%)
  matrix products  28.4 us (4%)
  local copies, waits for them, and re-layouts  18.6 us (3%)
  between operations  15 us (2%)
  starting transfers between devices  9.19 us (1%)
    reduce_scatter x1, waiting for transfers between devices, on_device(): lax.psum_scatter(lax.dot_general(gathered, kv_grad, (((0,), (0,)), ((), (...  352 us
    reduce_scatter x1, waiting for transfers between devices, on_device(): lax.psum_scatter(partial_value.astype(jnp.bfloat16), 'tensor', scatter_di...  125 us
    all_to_all x1, waiting for transfers between devices, on_device(): lax.all_to_all(jnp.stack([hidden] * lax.axis_size('tensor')), 'tensor', 0...  85.6 us
  transfers between devices with their start and end apart: 3, of which 3 were waited for; matrix products, arithmetic and copies ran while one was open for 3% of the time, Pallas kernels for 0%

profile of v1, /device:TPU:1, one launch (start us, length us, event | category | flops | bytes accessed | tf_op | source)
XLA Modules:
  0.0 635.3 jit_solution(8112992631194017726)
XLA Ops:
  7.2 2.9 copy.20
  10.0 3.9 stack.16
  13.9 9.0 %all-to-all-start = ((bf16[4,512,2048]{1,2,0:T(8,128)(2,1)}), bf16[4,512,2048]{1,2,0:T(8,128)(2,1)}, u32[]{:S(2)}, u32[]{:S(2)}) async-start(bf16[4,512,2048]{1,2,0:T(8,128)(2,1)} %stack.16), calls=%async_computation | async-start | bytes 16777216 | tf_op jit(solution)/shard_map/all_to_all | solution.py:59
  24.1 1.2 copy.50
  25.6 1.8 copy.51
  27.4 1.9 copy.27
  29.5 85.6 %all-to-all-done = bf16[4,512,2048]{1,2,0:T(8,128)(2,1)} async-done(((bf16[4,512,2048]{1,2,0:T(8,128)(2,1)}), bf16[4,512,2048]{1,2,0:T(8,128)(2,1)}, u32[]{:S(2)}, u32[]{:S(2)}) %all-to-all-start) | async-done | bytes 8388640 | tf_op jit(solution)/shard_map/all_to_all | solution.py:59
  115.1 7.7 %convolution_convert_fusion.3 = bf16[512,256]{1,0:T(8,128)(2,1)} fusion(bf16[512,8192]{0,1:T(8,128)(2,1)} %bitcast.1, bf16[8192,256]{1,0:T(8,128)(2,1)} %param.7), kind=kOutput, calls=%fused_computation.20 | convolution fusion | flops 2147614720 | bytes 12845056 | tf_op jit(solution)/shard_map/dot_general | solution.py:61
  122.8 1.0 reshape.132
  124.2 0.5 fusion.3
  124.7 0.5 fusion.7
  125.5 0.7 fusion.13
  126.2 0.8 fusion.8
  127.4 0.9 fusion.10
  128.4 0.4 fusion.14
  129.1 9.0 %convolution_bitcast_fusion = f32[8192,256]{0,1:T(8,128)} fusion(bf16[512,8192]{0,1:T(8,128)(2,1)} %bitcast.1, bf16[64,8,2,128]{3,2,1,0:T(2,128)(2,1)S(1)} %bitcast.155), kind=kOutput, calls=%fused_computation.1 | convolution fusion | flops 2147483648 | bytes 17039360 | tf_op jit(solution)/shard_map/dot_general | solution.py:83
  138.4 7.8 %convolution_convert_fusion = bf16[512,8192]{1,0:T(8,128)(2,1)} fusion(bf16[8192,256]{1,0:T(8,128)(2,1)} %param.7, bf16[64,8,2,128]{3,2,1,0:T(2,128)(2,1)S(1)} %bitcast.156), kind=kOutput, calls=%fused_computation | convolution fusion | flops 2151677952 | bytes 12845056 | tf_op jit(solution)/shard_map/dot_general | solution.py:76
  146.2 0.9 copy-done.4
  147.1 0.5 fusion.9
  147.6 0.7 copy.30
  148.3 1.2 copy.81
  149.6 351.9 %reduce-scatter.5.cloned.1.call-done = f32[128,256]{0,1:T(8,128)} async-done(((f32[8192,256]{0,1:T(8,128)}), f32[128,256]{0,1:T(8,128)}) %reduce-scatter.5.cloned.1.call-update) | async-done | bytes 131088 | tf_op jit(solution)/shard_map/reduce_scatter | solution.py:82
  501.5 1.7 copy.34
  503.2 125.3 %reduce-scatter.3.cloned.1.call-done = bf16[512,2048]{1,0:T(8,128)(2,1)} async-done(((bf16[512,8192]{1,0:T(8,128)(2,1)}), bf16[512,2048]{1,0:T(8,128)(2,1)}) %reduce-scatter.3.cloned.1.call-update) | async-done | bytes 2097168 | tf_op jit(solution)/shard_map/reduce_scatter | solution.py:79
  (25 shorter events, 2.4 us)
Async XLA Ops:
  13.9 9.7 %copy-start.1 = (bf16[512,1024]{1,0:T(8,128)(2,1)S(1)}, bf16[512,1024]{1,0:T(8,128)(2,1)}, u32[]{:S(2)}) copy-start(bf16[512,1024]{1,0:T(8,128)(2,1)} %param.8) | copy-start | bytes 3145732
  13.9 101.2 %all-to-all-start = ((bf16[4,512,2048]{1,2,0:T(8,128)(2,1)}), bf16[4,512,2048]{1,2,0:T(8,128)(2,1)}, u32[]{:S(2)}, u32[]{:S(2)}) async-start(bf16[4,512,2048]{1,2,0:T(8,128)(2,1)} %stack.16), calls=%async_computation | async-start | bytes 16777216 | tf_op jit(solution)/shard_map/all_to_all | solution.py:59
  22.9 1.2 copy-start
  22.9 478.6 %reduce-scatter.5.cloned.1.call-start = ((), (), s32[]{:S(2)}) async-start(), calls=%async_computation.4 | async-start | bytes 8519680 | tf_op jit(solution)/shard_map/reduce_scatter | solution.py:82
  27.4 2.0 copy-start.5
  124.2 1.0 copy-start.3
  124.2 1.3 copy-start.2
  138.1 490.3 %reduce-scatter.3.cloned.1.call-start = ((), (), s32[]{:S(2)}) async-start(), calls=%async_computation.3 | async-start | bytes 10485760 | tf_op jit(solution)/shard_map/reduce_scatter | solution.py:79
  146.2 0.9 copy-start.4
Sparse Core Ops, SparseCore 0:
  138.3 363.1 reduce-scatter.4
  504.7 123.7 reduce-scatter.2
